TPU v7x, 256 devices: a whole 4x4x8 slice. The times are simulated.
256 devices in a mesh: ctx: 32 (over z, y_hi, core), fsdp: 8 (over x, y_lo).
Axes of the slice: x: 4, y: 4 (y_hi: 2, y_lo: 2; y = y_hi * 2 + y_lo), z: 8, core: 2. Of those that a mesh axis runs over, the one named last changes fastest.
Arguments:
- xbc_raw: bfloat16 [8, 4096, 2560], P('fsdp', 'ctx'), may hold values from -6 to 6
- dt_raw: float32 [8, 4096, 64], P('fsdp', 'ctx'), as said below
- a_log: float32 [64], replicated, may hold values from 0 to 2.7726, as said below
- skip: float32 [64], replicated, may hold values from 0.5 to 1.5
- conv_weight: bfloat16 [4, 2560], P(None, 'fsdp'), may hold values from -3 to 3
- conv_bias: bfloat16 [2560], P('fsdp'), may hold values from -3 to 3
- grad_y: bfloat16 [8, 4096, 2048], P('fsdp', 'ctx'), may hold values from -6 to 6
Outputs:
- grad_xbc_raw: bfloat16 [8, 4096, 2560], P('fsdp', 'ctx')
- grad_dt_raw: float32 [8, 4096, 64], P('fsdp', 'ctx')
- grad_a_log: float32 [64], replicated
- grad_skip: float32 [64], replicated
- grad_conv_weight: float32 [4, 2560], P(None, 'fsdp')
- grad_conv_bias: float32 [2560], P('fsdp')
Inputs may be any that keep to these rules, and one draw needn't show every extreme that they name: Each head's decay coefficient exp(a_log) lies between 1 and 16. softplus(dt_raw) is a positive step size.
All inputs are finite; a program needn't handle non-finite values.
Results may differ from a plain program's by a relative error of at most 0.0007.
Values may be sent and summed in bfloat16 or wider, within the bound.
A program may use at most 256 MiB of HBM per device.

v0:
```python
import math
import jax
import jax.numpy as jnp
from jax import lax
from jax.sharding import PartitionSpec as P

HW = 64
GW = 4
P_SIZE = 32
N = 64
KW = 4
SPAN = 128
HIGHEST_PREC = lax.Precision.HIGHEST


def from_behind(value, axis, by):
    length = lax.axis_size(axis)
    pairs = [(i, i + by) for i in range(length) if 0 <= i + by < length]
    return lax.ppermute(value, axis, pairs)


def compose(earlier, later):
    return (earlier[0] * later[0], later[0][..., None, None] * earlier[1] + later[1])


def exclusive_scans(fwd, bwd, axis):
    count = lax.axis_size(axis)
    width = 1
    while 2 * width < count:
        fwd = compose(from_behind(fwd, axis, width), fwd)
        bwd = compose(from_behind(bwd, axis, -width), bwd)
        width *= 2
    fwd_near = from_behind(fwd, axis, 1)
    bwd_near = from_behind(bwd, axis, -1)
    if width + 1 < count:
        fwd = compose(from_behind(fwd, axis, width + 1), fwd_near)
        bwd = compose(from_behind(bwd, axis, -(width + 1)), bwd_near)
    else:
        fwd, bwd = (fwd_near, bwd_near)
    return (fwd[1], bwd[1])


def body(xbc_raw, dt_raw, a_log, skip, conv_weight, conv_bias, grad_y):
    raw_rows = xbc_raw[0]
    tok_rows = raw_rows.shape[0]
    per_group = HW // GW
    inner_width = HW * P_SIZE
    blocks = tok_rows // SPAN
    params_all = lax.all_gather(
        jnp.concatenate([conv_weight, conv_bias[None]], 0), "fsdp", axis=1, tiled=True
    ).astype(jnp.float32)
    weight_f = params_all[:KW]
    bias_f = params_all[KW]
    tail_rows = raw_rows[tok_rows - (KW - 1) :]
    rows_prev = from_behind(tail_rows, "ctx", 1)
    padded = jnp.concatenate([rows_prev, raw_rows], 0).astype(jnp.float32)
    pre_act = bias_f + sum(
        (weight_f[tap_idx] * padded[tap_idx : tap_idx + tok_rows] for tap_idx in range(KW))
    )
    gate_vals = jax.nn.sigmoid(pre_act)
    conv_out = pre_act * gate_vals
    x_all = conv_out[:, :inner_width].reshape(blocks, SPAN, GW, per_group, P_SIZE)
    b_all = conv_out[:, inner_width : inner_width + GW * N].reshape(blocks, SPAN, GW, N)
    c_all = conv_out[:, inner_width + GW * N :].reshape(blocks, SPAN, GW, N)
    steps_raw = dt_raw[0]
    step_size = jax.nn.softplus(steps_raw)
    rate_head = jnp.exp(a_log)
    log_decay = -rate_head * step_size
    dt_c = step_size.reshape(blocks, SPAN, GW, per_group)
    la_c = log_decay.reshape(blocks, SPAN, GW, per_group)
    d_out = grad_y[0].astype(jnp.float32).reshape(blocks, SPAN, GW, per_group, P_SIZE)
    cum_log = jnp.cumsum(la_c, 1)
    exp_cum = jnp.exp(cum_log)
    last_log = cum_log[:, -1]
    span_decay = jnp.exp(last_log)
    tail_decay = jnp.exp(last_log[:, None] - cum_log)
    inputs = dt_c[..., None] * x_all
    local_end = jnp.einsum(
        "csgkp,csgn->cgkpn", tail_decay[..., None] * inputs, b_all, precision=HIGHEST_PREC
    )
    local_adj = jnp.einsum(
        "ctgkp,ctgn->cgkpn", exp_cum[..., None] * d_out, c_all, precision=HIGHEST_PREC
    )
    unit_decay = jnp.ones((GW, per_group), jnp.float32)
    zero_state = jnp.zeros((GW, per_group, P_SIZE, N), jnp.float32)
    dev_decay = unit_decay
    fwd_total = zero_state
    span_idx = 0
    fwd_total = span_decay[span_idx][..., None, None] * fwd_total + local_end[span_idx]
    dev_decay = dev_decay * span_decay[span_idx]
    back_total = zero_state
    for span_idx in reversed(range(blocks)):
        back_total = local_adj[span_idx] + span_decay[span_idx][..., None, None] * back_total
    state_in, adjoint_end = exclusive_scans((dev_decay, fwd_total), (dev_decay, back_total), "ctx")
    cum_t = jnp.transpose(cum_log, (0, 2, 3, 1))
    lower_mask = jnp.tril(jnp.ones((SPAN, SPAN), bool))
    log_gap = cum_t[..., :, None] - cum_t[..., None, :]
    mixing = jnp.where(lower_mask, jnp.exp(jnp.where(lower_mask, log_gap, 0.0)), 0.0)
    scores = jnp.einsum("ctgn,csgn->cgts", c_all, b_all, precision=HIGHEST_PREC)
    weights = scores[:, :, None] * mixing
    d_weights = jnp.einsum("ctgkp,csgkp->cgkts", d_out, inputs, precision=HIGHEST_PREC)
    d_inputs = jnp.einsum("cgkts,ctgkp->csgkp", weights, d_out, precision=HIGHEST_PREC)
    flow_terms = d_weights * weights
    d_scores = jnp.sum(d_weights * mixing, 2)
    d_cum = jnp.transpose(jnp.sum(flow_terms, -1) - jnp.sum(flow_terms, -2), (0, 3, 1, 2))
    d_c = jnp.einsum("cgts,csgn->ctgn", d_scores, b_all, precision=HIGHEST_PREC)
    d_b = jnp.einsum("cgts,ctgn->csgn", d_scores, c_all, precision=HIGHEST_PREC)
    carried = state_in
    span_idx = 0
    start_list = [carried]
    end_list = []
    carried = adjoint_end
    for span_idx in reversed(range(blocks)):
        end_list.append(carried)
        carried = local_adj[span_idx] + span_decay[span_idx][..., None, None] * carried
    start_state = jnp.stack(start_list)
    end_adjoint = jnp.stack(end_list[::-1])
    from_state = jnp.einsum("ctgn,cgkpn->ctgkp", c_all, start_state, precision=HIGHEST_PREC)
    d_cum = d_cum + exp_cum * jnp.sum(d_out * from_state, -1)
    d_c = d_c + jnp.einsum(
        "ctgkp,cgkpn->ctgn", exp_cum[..., None] * d_out, start_state, precision=HIGHEST_PREC
    )
    pulled = jnp.einsum("cgkpn,csgn->csgkp", end_adjoint, b_all, precision=HIGHEST_PREC)
    d_inputs = d_inputs + tail_decay[..., None] * pulled
    d_b = d_b + jnp.einsum(
        "csgkp,cgkpn->csgn", tail_decay[..., None] * inputs, end_adjoint, precision=HIGHEST_PREC
    )
    d_tail = tail_decay * jnp.sum(inputs * pulled, -1)
    d_last = jnp.sum(d_tail, 1) + span_decay * jnp.sum(end_adjoint * start_state, (-2, -1))
    d_cum = d_cum - d_tail
    d_cum = d_cum.at[:, -1].add(d_last)
    d_log = jnp.flip(jnp.cumsum(jnp.flip(d_cum, 1), 1), 1)
    d_step = jnp.sum(d_inputs * x_all, -1) - rate_head.reshape(GW, per_group) * d_log
    d_x = d_inputs * dt_c[..., None] + skip.reshape(GW, per_group)[..., None] * d_out
    d_skip_local = jnp.sum(d_out * x_all, (0, 1, 4)).reshape(HW)
    d_alog_local = jnp.sum(d_log * la_c, (0, 1)).reshape(HW)
    d_dt_raw = d_step.reshape(tok_rows, HW) * jax.nn.sigmoid(steps_raw)
    d_conv = jnp.concatenate(
        [
            d_x.reshape(tok_rows, inner_width),
            d_b.reshape(tok_rows, GW * N),
            d_c.reshape(tok_rows, GW * N),
        ],
        1,
    )
    d_pre = d_conv * gate_vals * (1.0 + pre_act * (1.0 - gate_vals))
    rows_next = from_behind(d_pre[: KW - 1], "ctx", -1)
    extended = jnp.concatenate([d_pre, rows_next], 0)
    d_raw = sum(
        (
            weight_f[tap_idx] * extended[KW - 1 - tap_idx : KW - 1 - tap_idx + tok_rows]
            for tap_idx in range(KW)
        )
    )
    d_weight = jnp.stack(
        [jnp.sum(d_pre * padded[tap_idx : tap_idx + tok_rows], 0) for tap_idx in range(KW)]
    )
    d_bias = jnp.sum(d_pre, 0)
    grad_scale = 1.0 / math.sqrt(tok_rows * lax.axis_size("ctx") * lax.axis_size("fsdp"))
    channels = d_bias.shape[0]
    packed = jnp.concatenate([d_weight.reshape(-1), d_bias, d_alog_local, d_skip_local])
    packed = lax.psum(packed, ("ctx", "fsdp"))
    own = channels // lax.axis_size("fsdp")
    col0 = lax.axis_index("fsdp") * own
    wb = packed[: (KW + 1) * channels].reshape(KW + 1, channels)
    wb_own = lax.dynamic_slice_in_dim(wb, col0, own, axis=1)
    total_weight, total_bias = (wb_own[:KW], wb_own[KW])
    heads_part = packed[(KW + 1) * channels :]
    head_alog, head_skip = (heads_part[:HW], heads_part[HW:])
    return (
        d_raw.astype(jnp.bfloat16)[None],
        d_dt_raw[None],
        head_alog * grad_scale,
        head_skip * grad_scale,
        total_weight * grad_scale,
        total_bias * grad_scale,
    )


def solution(mesh):
    in_specs = (
        P("fsdp", "ctx", None),
        P("fsdp", "ctx", None),
        P(),
        P(),
        P(None, "fsdp"),
        P("fsdp"),
        P("fsdp", "ctx", None),
    )
    out_specs = (
        P("fsdp", "ctx", None),
        P("fsdp", "ctx", None),
        P(),
        P(),
        P(None, "fsdp"),
        P("fsdp"),
    )
    return jax.shard_map(body, mesh=mesh, in_specs=in_specs, out_specs=out_specs, check_vma=False)
```

profile of v0, /device:TPU:1, one launch (start us, length us, event | category | flops | bytes accessed | tf_op | source)
XLA Modules:
  0.0 447.0 jit_solution(13302643420018480362)
XLA Ops:
  3.4 5.1 %collective-permute-start.1 = (f32[4,16]{1,0:T(4,128)S(1)}, f32[4,16]{1,0:T(4,128)S(1)}, u32[]{:S(2)}, u32[]{:S(2)}) collective-permute-start(f32[4,16]{1,0:T(4,128)S(1)} %exp.91), channel_id=1, source_target_pairs={{8,0},{16,8},{24,16},{32,24},{40,32},{48,40},{56,48},{64,56},{72,6... | collective-permute-start | bytes 776 | tf_op jit(solution)/shard_map/ppermute | solution.py:19
  15.4 22.3 %all-gather = bf16[8,320,5]{1,2,0:T(8,128)(2,1)S(1)} all-gather(bf16[1,320,5]{1,2,0:T(8,128)(2,1)S(1)} %maximum_bitcast_fusion), channel_id=1, replica_groups=mesh['ctx'=32,'fsdp'=8] {'fsdp'}, dimensions={0}, use_global_device_ids=true | all-gather | bytes 28800 | tf_op jit(solution)/shard_map/all_gather | solution.py:49
  43.1 4.0 fusion.25
  49.1 11.6 %collective-permute-start.17 = (f32[4,16,32,64]{3,2,1,0:T(8,128)S(1)}, f32[4,16,32,64]{3,2,1,0:T(8,128)S(1)}, u32[]{:S(2)}, u32[]{:S(2)}) collective-permute-start(f32[4,16,32,64]{3,2,1,0:T(8,128)S(1)} %convolution_add_fusion), channel_id=1, source_target_pairs={{0,8},{8,16},{16,24},{24,32},{32,40},{40,48},{48,56},{56,64},{64,7... | collective-permute-start | bytes 1572872 | tf_op jit(solution)/shard_map/ppermute | solution.py:19
  63.7 19.9 %collective-permute-done.17 = f32[4,16,32,64]{3,2,1,0:T(8,128)S(1)} collective-permute-done((f32[4,16,32,64]{3,2,1,0:T(8,128)S(1)}, f32[4,16,32,64]{3,2,1,0:T(8,128)S(1)}, u32[]{:S(2)}, u32[]{:S(2)}) %collective-permute-start.17) | collective-permute-done | bytes 524320 | tf_op jit(solution)/shard_map/ppermute | solution.py:19
  93.8 7.8 %collective-permute-start.13 = (f32[4,16]{1,0:T(4,128)}, f32[4,16]{1,0:T(4,128)}, u32[]{:S(2)}, u32[]{:S(2)}) collective-permute-start(f32[4,16]{1,0:T(4,128)} %get-tuple-element.83), channel_id=1, source_target_pairs={{0,16},{8,24},{16,32},{24,40},{32,48},{40,56},{48,64},{56,72},{64,... | collective-permute-start | bytes 776 | tf_op jit(solution)/shard_map/ppermute | solution.py:19
  102.9 24.3 %collective-permute-done.13 = f32[4,16]{1,0:T(4,128)} collective-permute-done((f32[4,16]{1,0:T(4,128)}, f32[4,16]{1,0:T(4,128)}, u32[]{:S(2)}, u32[]{:S(2)}) %collective-permute-start.13) | collective-permute-done | bytes 288 | tf_op jit(solution)/shard_map/ppermute | solution.py:19
  128.4 6.8 %collective-permute-start.14 = (f32[4,16]{1,0:T(4,128)}, f32[4,16]{1,0:T(4,128)}, u32[]{:S(2)}, u32[]{:S(2)}) collective-permute-start(f32[4,16]{1,0:T(4,128)} %mul.469), channel_id=1, source_target_pairs={{0,32},{8,40},{16,48},{24,56},{32,64},{40,72},{48,80},{56,88},{64,... | collective-permute-start | bytes 776 | tf_op jit(solution)/shard_map/ppermute | solution.py:19
  139.1 8.3 %collective-permute-start.15 = (f32[4,16]{1,0:T(4,128)}, f32[4,16]{1,0:T(4,128)}, u32[]{:S(2)}, u32[]{:S(2)}) collective-permute-start(f32[4,16]{1,0:T(4,128)} %mul.470), channel_id=1, source_target_pairs={{0,64},{8,72},{16,80},{24,88},{32,96},{40,104},{48,112},{56,120},{... | collective-permute-start | bytes 776 | tf_op jit(solution)/shard_map/ppermute | solution.py:19
  150.7 8.0 %collective-permute-start.16 = (f32[4,16]{1,0:T(4,128)S(1)}, f32[4,16]{1,0:T(4,128)}, u32[]{:S(2)}, u32[]{:S(2)}) collective-permute-start(f32[4,16]{1,0:T(4,128)S(1)} %mul.471), channel_id=1, source_target_pairs={{0,8},{8,16},{16,24},{24,32},{32,40},{40,48},{48,56},{56,64},{64,7... | collective-permute-start | bytes 776 | tf_op jit(solution)/shard_map/ppermute | solution.py:19
  161.7 5.5 %collective-permute-start.19 = (f32[4,16,32,64]{3,2,1,0:T(8,128)S(1)}, f32[4,16,32,64]{3,2,1,0:T(8,128)S(1)}, u32[]{:S(2)}, u32[]{:S(2)}) collective-permute-start(f32[4,16,32,64]{3,2,1,0:T(8,128)S(1)} %multiply_add_fusion.3), channel_id=1, source_target_pairs={{0,32},{8,40},{16,48},{24,56},{32,64},{40,72},{48,80},{56,88},{64,... | collective-permute-start | bytes 1572872 | tf_op jit(solution)/shard_map/ppermute | solution.py:19
  170.8 18.9 %collective-permute-done.19 = f32[4,16,32,64]{3,2,1,0:T(8,128)S(1)} collective-permute-done((f32[4,16,32,64]{3,2,1,0:T(8,128)S(1)}, f32[4,16,32,64]{3,2,1,0:T(8,128)S(1)}, u32[]{:S(2)}, u32[]{:S(2)}) %collective-permute-start.19) | collective-permute-done | bytes 524320 | tf_op jit(solution)/shard_map/ppermute | solution.py:19
  190.6 7.2 %collective-permute-start.20 = (f32[4,16,32,64]{3,2,1,0:T(8,128)S(1)}, f32[4,16,32,64]{3,2,1,0:T(8,128)S(1)}, u32[]{:S(2)}, u32[]{:S(2)}) collective-permute-start(f32[4,16,32,64]{3,2,1,0:T(8,128)S(1)} %multiply_add_fusion.2), channel_id=1, source_target_pairs={{0,64},{8,72},{16,80},{24,88},{32,96},{40,104},{48,112},{56,120},{... | collective-permute-start | bytes 1572872 | tf_op jit(solution)/shard_map/ppermute | solution.py:19
  200.0 6.6 %fusion.4 = (f32[4,16,128]{2,1,0:T(8,128)}, f32[4,16,128]{2,1,0:T(8,128)}, f32[4,128,128]{1,2,0:T(8,128)S(1)}) fusion(f32[4,16,128]{2,1,0:T(8,128)S(1)} %copy-done.24, f32[4,128,128]{1,2,0:T(8,128)S(1)} %fusion.54, pred[128,128]{0,1:T(8,128)(4,1)S(1)} %copy-done.31, bf16[128,4,16,32]{0,3,2,1:T(8,128)(2,1)S(1)} %bitcast.135, ...), kind=kOutput, calls=%fused_computation.10 | convolution fusion | flops 412270592 | bytes 2244608 | tf_op jit(solution)/shard_map/ctgkp,csgkp->cgkts/dot_general | solution.py:101
  206.6 13.1 %collective-permute-done.20 = f32[4,16,32,64]{3,2,1,0:T(8,128)S(1)} collective-permute-done((f32[4,16,32,64]{3,2,1,0:T(8,128)S(1)}, f32[4,16,32,64]{3,2,1,0:T(8,128)S(1)}, u32[]{:S(2)}, u32[]{:S(2)}) %collective-permute-start.20) | collective-permute-done | bytes 524320 | tf_op jit(solution)/shard_map/ppermute | solution.py:19
  221.6 10.7 %collective-permute-start.21 = (f32[4,16,32,64]{3,2,1,0:T(8,128)}, f32[4,16,32,64]{3,2,1,0:T(8,128)}, u32[]{:S(2)}, u32[]{:S(2)}) collective-permute-start(f32[4,16,32,64]{3,2,1,0:T(8,128)} %multiply_add_fusion.1), channel_id=1, source_target_pairs={{0,136},{8,144},{16,152},{24,160},{32,168},{40,176},{48,184},{56,1... | collective-permute-start | bytes 1572872 | tf_op jit(solution)/shard_map/ppermute | solution.py:19
  234.2 12.7 %collective-permute-done.9 = f32[4,16,32,64]{3,2,1,0:T(8,128)S(1)} collective-permute-done((f32[4,16,32,64]{3,2,1,0:T(8,128)S(1)}, f32[4,16,32,64]{3,2,1,0:T(8,128)S(1)}, u32[]{:S(2)}, u32[]{:S(2)}) %collective-permute-start.9) | collective-permute-done | bytes 524320 | tf_op jit(solution)/shard_map/ppermute | solution.py:19
  253.1 5.0 %fusion.11 = f32[1,128,4,16,32]{1,4,3,2,0:T(8,128)} fusion(bf16[128,4,16,32]{0,3,2,1:T(8,128)(2,1)S(1)} %bitcast.136, f32[4,16,128]{2,1,0:T(8,128)S(1)} %copy-done.24, f32[4,128,128]{1,2,0:T(8,128)S(1)} %fusion.54, pred[128,128]{0,1:T(8,128)(4,1)S(1)} %copy-done.31), kind=kOutput, calls=%fused_computation.17 | convolution fusion | flops 406847488 | bytes 1884160 | tf_op jit(solution)/shard_map/cgkts,ctgkp->csgkp/dot_general | solution.py:102
  266.4 41.0 %collective-permute-done.5 = f32[4,16]{1,0:T(4,128)} collective-permute-done((f32[4,16]{1,0:T(4,128)}, f32[4,16]{1,0:T(4,128)}, u32[]{:S(2)}, u32[]{:S(2)}) %collective-permute-start.5) | collective-permute-done | bytes 288 | tf_op jit(solution)/shard_map/ppermute | solution.py:19
  307.4 3.3 multiply_reduce_fusion.4
  314.7 3.1 multiply_reduce_fusion.5
  317.7 4.2 multiply_reduce_fusion.3
  326.8 106.5 %psum.7 = f32[12928]{0:T(1024)S(1)} all-reduce(f32[12928]{0:T(1024)S(1)} %concatenate.21), channel_id=1, replica_groups=mesh['ctx'=32,'fsdp'=8] {'ctx','fsdp'}, use_global_device_ids=true, to_apply=%region_18.19 | all-reduce | flops 12928 | bytes 103424 | tf_op jit(solution)/shard_map/psum | solution.py:162
  442.2 3.7 fusion.36
  (192 shorter events, 85.8 us)
Async XLA Ops:
  3.4 36.0 %collective-permute-start.1 = (f32[4,16]{1,0:T(4,128)S(1)}, f32[4,16]{1,0:T(4,128)S(1)}, u32[]{:S(2)}, u32[]{:S(2)}) collective-permute-start(f32[4,16]{1,0:T(4,128)S(1)} %exp.91), channel_id=1, source_target_pairs={{8,0},{16,8},{24,16},{32,24},{40,32},{48,40},{56,48},{64,56},{72,6... | collective-permute-start | bytes 776 | tf_op jit(solution)/shard_map/ppermute | solution.py:19
  8.5 30.9 %collective-permute-start.12 = (f32[4,16]{1,0:T(4,128)S(1)}, f32[4,16]{1,0:T(4,128)S(1)}, u32[]{:S(2)}, u32[]{:S(2)}) collective-permute-start(f32[4,16]{1,0:T(4,128)S(1)} %exp.91), channel_id=1, source_target_pairs={{0,8},{8,16},{16,24},{24,32},{32,40},{40,48},{48,56},{56,64},{64,7... | collective-permute-start | bytes 776 | tf_op jit(solution)/shard_map/ppermute | solution.py:19
  12.4 27.7 %collective-permute-start = (bf16[3,2560]{1,0:T(4,128)(2,1)S(1)}, bf16[3,2560]{1,0:T(4,128)(2,1)S(1)}, u32[]{:S(2)}, u32[]{:S(2)}) collective-permute-start(bf16[3,2560]{1,0:T(4,128)(2,1)S(1)} %slice_bitcast_fusion), channel_id=1, source_target_pairs={{0,8},{8,16},{16,24},{24,32},{32,40},{40,48},{48,56},{56,64},{64,7... | collective-permute-start | bytes 46088 | tf_op jit(solution)/shard_map/ppermute | solution.py:19
  49.1 34.5 %collective-permute-start.17 = (f32[4,16,32,64]{3,2,1,0:T(8,128)S(1)}, f32[4,16,32,64]{3,2,1,0:T(8,128)S(1)}, u32[]{:S(2)}, u32[]{:S(2)}) collective-permute-start(f32[4,16,32,64]{3,2,1,0:T(8,128)S(1)} %convolution_add_fusion), channel_id=1, source_target_pairs={{0,8},{8,16},{16,24},{24,32},{32,40},{40,48},{48,56},{56,64},{64,7... | collective-permute-start | bytes 1572872 | tf_op jit(solution)/shard_map/ppermute | solution.py:19
  61.8 21.9 %collective-permute-start.6 = (f32[4,16,32,64]{3,2,1,0:T(8,128)S(1)}, f32[4,16,32,64]{3,2,1,0:T(8,128)S(1)}, u32[]{:S(2)}, u32[]{:S(2)}) collective-permute-start(f32[4,16,32,64]{3,2,1,0:T(8,128)S(1)} %convolution_add_fusion.1), channel_id=1, source_target_pairs={{8,0},{16,8},{24,16},{32,24},{40,32},{48,40},{56,48},{64,56},{72,6... | collective-permute-start | bytes 1572872 | tf_op jit(solution)/shard_map/ppermute | solution.py:19
  85.3 74.7 %collective-permute-start.18 = (f32[4,16,32,64]{3,2,1,0:T(8,128)}, f32[4,16,32,64]{3,2,1,0:T(8,128)}, u32[]{:S(2)}, u32[]{:S(2)}) collective-permute-start(f32[4,16,32,64]{3,2,1,0:T(8,128)} %get-tuple-element.86), channel_id=1, source_target_pairs={{0,16},{8,24},{16,32},{24,40},{32,48},{40,56},{48,64},{56,72},{64,... | collective-permute-start | bytes 1572872 | tf_op jit(solution)/shard_map/ppermute | solution.py:19
  87.6 79.6 %collective-permute-start.7 = (f32[4,16,32,64]{3,2,1,0:T(8,128)}, f32[4,16,32,64]{3,2,1,0:T(8,128)}, u32[]{:S(2)}, u32[]{:S(2)}) collective-permute-start(f32[4,16,32,64]{3,2,1,0:T(8,128)} %get-tuple-element.87), channel_id=1, source_target_pairs={{16,0},{24,8},{32,16},{40,24},{48,32},{56,40},{64,48},{72,56},{80,... | collective-permute-start | bytes 1572872 | tf_op jit(solution)/shard_map/ppermute | solution.py:19
  93.8 33.4 %collective-permute-start.13 = (f32[4,16]{1,0:T(4,128)}, f32[4,16]{1,0:T(4,128)}, u32[]{:S(2)}, u32[]{:S(2)}) collective-permute-start(f32[4,16]{1,0:T(4,128)} %get-tuple-element.83), channel_id=1, source_target_pairs={{0,16},{8,24},{16,32},{24,40},{32,48},{40,56},{48,64},{56,72},{64,... | collective-permute-start | bytes 776 | tf_op jit(solution)/shard_map/ppermute | solution.py:19
  101.6 33.7 %collective-permute-start.2 = (f32[4,16]{1,0:T(4,128)}, f32[4,16]{1,0:T(4,128)}, u32[]{:S(2)}, u32[]{:S(2)}) collective-permute-start(f32[4,16]{1,0:T(4,128)} %get-tuple-element.84), channel_id=1, source_target_pairs={{16,0},{24,8},{32,16},{40,24},{48,32},{56,40},{64,48},{72,56},{80,... | collective-permute-start | bytes 776 | tf_op jit(solution)/shard_map/ppermute | solution.py:19
  128.4 9.4 %collective-permute-start.14 = (f32[4,16]{1,0:T(4,128)}, f32[4,16]{1,0:T(4,128)}, u32[]{:S(2)}, u32[]{:S(2)}) collective-permute-start(f32[4,16]{1,0:T(4,128)} %mul.469), channel_id=1, source_target_pairs={{0,32},{8,40},{16,48},{24,56},{32,64},{40,72},{48,80},{56,88},{64,... | collective-permute-start | bytes 776 | tf_op jit(solution)/shard_map/ppermute | solution.py:19
  136.5 10.9 %collective-permute-start.3 = (f32[4,16]{1,0:T(4,128)}, f32[4,16]{1,0:T(4,128)}, u32[]{:S(2)}, u32[]{:S(2)}) collective-permute-start(f32[4,16]{1,0:T(4,128)} %mul.440), channel_id=1, source_target_pairs={{32,0},{40,8},{48,16},{56,24},{64,32},{72,40},{80,48},{88,56},{96,... | collective-permute-start | bytes 776 | tf_op jit(solution)/shard_map/ppermute | solution.py:19
  139.1 10.9 %collective-permute-start.15 = (f32[4,16]{1,0:T(4,128)}, f32[4,16]{1,0:T(4,128)}, u32[]{:S(2)}, u32[]{:S(2)}) collective-permute-start(f32[4,16]{1,0:T(4,128)} %mul.470), channel_id=1, source_target_pairs={{0,64},{8,72},{16,80},{24,88},{32,96},{40,104},{48,112},{56,120},{... | collective-permute-start | bytes 776 | tf_op jit(solution)/shard_map/ppermute | solution.py:19
  148.7 10.0 %collective-permute-start.4 = (f32[4,16]{1,0:T(4,128)}, f32[4,16]{1,0:T(4,128)}, u32[]{:S(2)}, u32[]{:S(2)}) collective-permute-start(f32[4,16]{1,0:T(4,128)} %mul.441), channel_id=1, source_target_pairs={{64,0},{72,8},{80,16},{88,24},{96,32},{104,40},{112,48},{120,56},{... | collective-permute-start | bytes 776 | tf_op jit(solution)/shard_map/ppermute | solution.py:19
  150.7 109.7 %collective-permute-start.16 = (f32[4,16]{1,0:T(4,128)S(1)}, f32[4,16]{1,0:T(4,128)}, u32[]{:S(2)}, u32[]{:S(2)}) collective-permute-start(f32[4,16]{1,0:T(4,128)S(1)} %mul.471), channel_id=1, source_target_pairs={{0,8},{8,16},{16,24},{24,32},{32,40},{40,48},{48,56},{56,64},{64,7... | collective-permute-start | bytes 776 | tf_op jit(solution)/shard_map/ppermute | solution.py:19
  161.7 28.1 %collective-permute-start.19 = (f32[4,16,32,64]{3,2,1,0:T(8,128)S(1)}, f32[4,16,32,64]{3,2,1,0:T(8,128)S(1)}, u32[]{:S(2)}, u32[]{:S(2)}) collective-permute-start(f32[4,16,32,64]{3,2,1,0:T(8,128)S(1)} %multiply_add_fusion.3), channel_id=1, source_target_pairs={{0,32},{8,40},{16,48},{24,56},{32,64},{40,72},{48,80},{56,88},{64,... | collective-permute-start | bytes 1572872 | tf_op jit(solution)/shard_map/ppermute | solution.py:19
  168.9 28.9 %collective-permute-start.8 = (f32[4,16,32,64]{3,2,1,0:T(8,128)S(1)}, f32[4,16,32,64]{3,2,1,0:T(8,128)S(1)}, u32[]{:S(2)}, u32[]{:S(2)}) collective-permute-start(f32[4,16,32,64]{3,2,1,0:T(8,128)S(1)} %multiply_add_fusion.10), channel_id=1, source_target_pairs={{32,0},{40,8},{48,16},{56,24},{64,32},{72,40},{80,48},{88,56},{96,... | collective-permute-start | bytes 1572872 | tf_op jit(solution)/shard_map/ppermute | solution.py:19
  190.6 29.1 %collective-permute-start.20 = (f32[4,16,32,64]{3,2,1,0:T(8,128)S(1)}, f32[4,16,32,64]{3,2,1,0:T(8,128)S(1)}, u32[]{:S(2)}, u32[]{:S(2)}) collective-permute-start(f32[4,16,32,64]{3,2,1,0:T(8,128)S(1)} %multiply_add_fusion.2), channel_id=1, source_target_pairs={{0,64},{8,72},{16,80},{24,88},{32,96},{40,104},{48,112},{56,120},{... | collective-permute-start | bytes 1572872 | tf_op jit(solution)/shard_map/ppermute | solution.py:19
  198.7 48.2 %collective-permute-start.9 = (f32[4,16,32,64]{3,2,1,0:T(8,128)S(1)}, f32[4,16,32,64]{3,2,1,0:T(8,128)S(1)}, u32[]{:S(2)}, u32[]{:S(2)}) collective-permute-start(f32[4,16,32,64]{3,2,1,0:T(8,128)S(1)} %multiply_add_fusion.9), channel_id=1, source_target_pairs={{64,0},{72,8},{80,16},{88,24},{96,32},{104,40},{112,48},{120,56},{... | collective-permute-start | bytes 1572872 | tf_op jit(solution)/shard_map/ppermute | solution.py:19
  221.6 85.8 %collective-permute-start.21 = (f32[4,16,32,64]{3,2,1,0:T(8,128)}, f32[4,16,32,64]{3,2,1,0:T(8,128)}, u32[]{:S(2)}, u32[]{:S(2)}) collective-permute-start(f32[4,16,32,64]{3,2,1,0:T(8,128)} %multiply_add_fusion.1), channel_id=1, source_target_pairs={{0,136},{8,144},{16,152},{24,160},{32,168},{40,176},{48,184},{56,1... | collective-permute-start | bytes 1572872 | tf_op jit(solution)/shard_map/ppermute | solution.py:19
  232.2 75.1 %collective-permute-start.22 = (f32[4,16,32,64]{3,2,1,0:T(8,128)}, f32[4,16,32,64]{3,2,1,0:T(8,128)}, u32[]{:S(2)}, u32[]{:S(2)}) collective-permute-start(f32[4,16,32,64]{3,2,1,0:T(8,128)} %multiply_add_fusion.1), channel_id=1, source_target_pairs={{0,8},{8,16},{16,24},{24,32},{32,40},{40,48},{48,56},{56,64},{64,7... | collective-permute-start | bytes 1572872 | tf_op jit(solution)/shard_map/ppermute | solution.py:19
  248.8 58.6 %collective-permute-start.10 = (f32[4,16,32,64]{3,2,1,0:T(8,128)}, f32[4,16,32,64]{3,2,1,0:T(8,128)}, u32[]{:S(2)}, u32[]{:S(2)}) collective-permute-start(f32[4,16,32,64]{3,2,1,0:T(8,128)} %multiply_add_fusion.8), channel_id=1, source_target_pairs={{136,0},{144,8},{152,16},{160,24},{168,32},{176,40},{184,48},{192,... | collective-permute-start | bytes 1572872 | tf_op jit(solution)/shard_map/ppermute | solution.py:19
  250.1 57.3 %collective-permute-start.11 = (f32[4,16,32,64]{3,2,1,0:T(8,128)}, f32[4,16,32,64]{3,2,1,0:T(8,128)}, u32[]{:S(2)}, u32[]{:S(2)}) collective-permute-start(f32[4,16,32,64]{3,2,1,0:T(8,128)} %multiply_add_fusion.8), channel_id=1, source_target_pairs={{8,0},{16,8},{24,16},{32,24},{40,32},{48,40},{56,48},{64,56},{72,6... | collective-permute-start | bytes 1572872 | tf_op jit(solution)/shard_map/ppermute | solution.py:19
  260.4 47.0 %collective-permute-start.5 = (f32[4,16]{1,0:T(4,128)}, f32[4,16]{1,0:T(4,128)}, u32[]{:S(2)}, u32[]{:S(2)}) collective-permute-start(f32[4,16]{1,0:T(4,128)} %mul.442), channel_id=1, source_target_pairs={{8,0},{16,8},{24,16},{32,24},{40,32},{48,40},{56,48},{64,56},{72,6... | collective-permute-start | bytes 776 | tf_op jit(solution)/shard_map/ppermute | solution.py:19
  434.9 6.8 %collective-permute-start.23 = (f32[3,2560]{1,0:T(4,128)S(1)}, f32[3,2560]{1,0:T(4,128)S(1)}, u32[]{:S(2)}, u32[]{:S(2)}) collective-permute-start(f32[3,2560]{1,0:T(4,128)S(1)} %copy.147), channel_id=1, source_target_pairs={{8,0},{16,8},{24,16},{32,24},{40,32},{48,40},{56,48},{64,56},{72,6... | collective-permute-start | bytes 92168 | tf_op jit(solution)/shard_map/ppermute | solution.py:19
  (40 other events, 594.5 us)
where the time goes:
time: 449 us; the launch traced here: 447 us
  waiting for transfers between devices  133 us (30%)
  blocking collectives  129 us (29%)
  starting transfers between devices  99.2 us (22%)
  other arithmetic  44.1 us (10%)
  matrix products  26.2 us (6%)
  local copies, waits for them, and re-layouts  14.5 us (3%)
    ppermute x24, waiting for transfers between devices, from_behind(): return lax.ppermute(value, axis, pairs)  133 us
    psum x1, blocking collectives, body(): packed = lax.psum(packed, ('ctx', 'fsdp'))  107 us
    ppermute x24, starting transfers between devices, from_behind(): return lax.ppermute(value, axis, pairs)  99.2 us
    all_gather x1, blocking collectives, body(): lax.all_gather(jnp.concatenate([conv_weight, conv_bias[None]], 0), 'fsdp'...  22.3 us
    add x7, other arithmetic, compose(): later[0][..., None, None] * earlier[1] + later[1]  10.5 us
  transfers between devices with their start and end apart: 24, of which 7 were waited for; matrix products, arithmetic and copies ran while one was open for 10% of the time, Pallas kernels for 0%

commit v1 on v0

--- a/solution.py
+++ b/solution.py
@@ -46,8 +46,14 @@
     per_group = HW // GW
     inner_width = HW * P_SIZE
     blocks = tok_rows // SPAN
-    params_all = lax.all_gather(
-        jnp.concatenate([conv_weight, conv_bias[None]], 0), "fsdp", axis=1, tiled=True
+    params_all = jnp.concatenate(
+        lax.all_to_all(
+            jnp.stack([jnp.concatenate([conv_weight, conv_bias[None]], 0)] * lax.axis_size("fsdp")),
+            "fsdp",
+            0,
+            0,
+        ),
+        axis=1,
     ).astype(jnp.float32)
     weight_f = params_all[:KW]
     bias_f = params_all[KW]

time: 449 us -> 430 us (0.958)
  blocking collectives: 129 us -> 107 us
    all_gather x1 -> x0, blocking collectives: 22.3 us -> none  [body(): lax.all_gather(jnp.concatenate([conv_weight, conv_bias[None]], 0), 'fsdp'...]
    all_to_all x0 -> x1, starting transfers between devices: none -> 4.8 us  [body(): lax.all_to_all(jnp.stack([jnp.concatenate([conv_weight, conv_bias[None]],...]
  transfers between devices with their start and end apart: 24 -> 25, of which waited for: 7 -> 8; matrix products, arithmetic and copies ran while one was open for 10% -> 12% of each run, Pallas kernels for 0% -> 0%
where the time goes in v1:
time: 430 us; the launch traced here: 428 us
  waiting for transfers between devices  132 us (31%)
  blocking collectives  107 us (25%)
  starting transfers between devices  102 us (24%)
  other arithmetic  44.7 us (10%)
  matrix products  26.2 us (6%)
  local copies, waits for them, and re-layouts  15.3 us (4%)
    ppermute x24, waiting for transfers between devices, from_behind(): return lax.ppermute(value, axis, pairs)  132 us
    psum x1, blocking collectives, body(): packed = lax.psum(packed, ('ctx', 'fsdp'))  107 us
    ppermute x24, starting transfers between devices, from_behind(): return lax.ppermute(value, axis, pairs)  96.9 us
    add x7, other arithmetic, compose(): later[0][..., None, None] * earlier[1] + later[1]  10.5 us
  transfers between devices with their start and end apart: 25, of which 8 were waited for; matrix products, arithmetic and copies ran while one was open for 12% of the time, Pallas kernels for 0%

profile of v1, /device:TPU:1, one launch (start us, length us, event | category | flops | bytes accessed | tf_op | source)
XLA Modules:
  0.0 428.1 jit_solution(7634683368839689635)
XLA Ops:
  3.4 5.1 %collective-permute-start.1 = (f32[4,16]{1,0:T(4,128)S(1)}, f32[4,16]{1,0:T(4,128)S(1)}, u32[]{:S(2)}, u32[]{:S(2)}) collective-permute-start(f32[4,16]{1,0:T(4,128)S(1)} %exp.91), channel_id=1, source_target_pairs={{8,0},{16,8},{24,16},{32,24},{40,32},{48,40},{56,48},{64,56},{72,6... | collective-permute-start | bytes 776 | tf_op jit(solution)/shard_map/ppermute | solution.py:19
  13.6 4.8 %all-to-all-start = ((bf16[8,5,320]{2,1,0:T(8,128)(2,1)}), bf16[8,5,320]{2,1,0:T(8,128)(2,1)S(1)}, u32[]{:S(2)}, u32[]{:S(2)}) async-start(bf16[8,5,320]{2,1,0:T(8,128)(2,1)} %stack.12), calls=%async_computation | async-start | bytes 98304 | tf_op jit(solution)/shard_map/all_to_all | solution.py:50
  27.4 3.9 fusion.25
  33.4 4.9 %collective-permute-start.17 = (f32[4,16,32,64]{3,2,1,0:T(8,128)S(1)}, f32[4,16,32,64]{3,2,1,0:T(8,128)S(1)}, u32[]{:S(2)}, u32[]{:S(2)}) collective-permute-start(f32[4,16,32,64]{3,2,1,0:T(8,128)S(1)} %convolution_add_fusion), channel_id=1, source_target_pairs={{0,8},{8,16},{16,24},{24,32},{32,40},{40,48},{48,56},{56,64},{64,7... | collective-permute-start | bytes 1572872 | tf_op jit(solution)/shard_map/ppermute | solution.py:19
  41.4 19.9 %collective-permute-done.17 = f32[4,16,32,64]{3,2,1,0:T(8,128)S(1)} collective-permute-done((f32[4,16,32,64]{3,2,1,0:T(8,128)S(1)}, f32[4,16,32,64]{3,2,1,0:T(8,128)S(1)}, u32[]{:S(2)}, u32[]{:S(2)}) %collective-permute-start.17) | collective-permute-done | bytes 524320 | tf_op jit(solution)/shard_map/ppermute | solution.py:19
  71.5 9.6 %collective-permute-start.13 = (f32[4,16]{1,0:T(4,128)}, f32[4,16]{1,0:T(4,128)}, u32[]{:S(2)}, u32[]{:S(2)}) collective-permute-start(f32[4,16]{1,0:T(4,128)} %get-tuple-element.83), channel_id=1, source_target_pairs={{0,16},{8,24},{16,32},{24,40},{32,48},{40,56},{48,64},{56,72},{64,... | collective-permute-start | bytes 776 | tf_op jit(solution)/shard_map/ppermute | solution.py:19
  82.3 22.5 %collective-permute-done.13 = f32[4,16]{1,0:T(4,128)} collective-permute-done((f32[4,16]{1,0:T(4,128)}, f32[4,16]{1,0:T(4,128)}, u32[]{:S(2)}, u32[]{:S(2)}) %collective-permute-start.13) | collective-permute-done | bytes 288 | tf_op jit(solution)/shard_map/ppermute | solution.py:19
  106.1 10.4 %collective-permute-start.14 = (f32[4,16]{1,0:T(4,128)}, f32[4,16]{1,0:T(4,128)}, u32[]{:S(2)}, u32[]{:S(2)}) collective-permute-start(f32[4,16]{1,0:T(4,128)} %mul.469), channel_id=1, source_target_pairs={{0,32},{8,40},{16,48},{24,56},{32,64},{40,72},{48,80},{56,88},{64,... | collective-permute-start | bytes 776 | tf_op jit(solution)/shard_map/ppermute | solution.py:19
  120.4 5.3 %collective-permute-start.15 = (f32[4,16]{1,0:T(4,128)}, f32[4,16]{1,0:T(4,128)}, u32[]{:S(2)}, u32[]{:S(2)}) collective-permute-start(f32[4,16]{1,0:T(4,128)} %mul.470), channel_id=1, source_target_pairs={{0,64},{8,72},{16,80},{24,88},{32,96},{40,104},{48,112},{56,120},{... | collective-permute-start | bytes 776 | tf_op jit(solution)/shard_map/ppermute | solution.py:19
  129.0 9.1 %collective-permute-start.16 = (f32[4,16]{1,0:T(4,128)S(1)}, f32[4,16]{1,0:T(4,128)}, u32[]{:S(2)}, u32[]{:S(2)}) collective-permute-start(f32[4,16]{1,0:T(4,128)S(1)} %mul.471), channel_id=1, source_target_pairs={{0,8},{8,16},{16,24},{24,32},{32,40},{40,48},{48,56},{56,64},{64,7... | collective-permute-start | bytes 776 | tf_op jit(solution)/shard_map/ppermute | solution.py:19
  142.0 5.9 %collective-permute-start.19 = (f32[4,16,32,64]{3,2,1,0:T(8,128)S(1)}, f32[4,16,32,64]{3,2,1,0:T(8,128)S(1)}, u32[]{:S(2)}, u32[]{:S(2)}) collective-permute-start(f32[4,16,32,64]{3,2,1,0:T(8,128)S(1)} %multiply_add_fusion.3), channel_id=1, source_target_pairs={{0,32},{8,40},{16,48},{24,56},{32,64},{40,72},{48,80},{56,88},{64,... | collective-permute-start | bytes 1572872 | tf_op jit(solution)/shard_map/ppermute | solution.py:19
  151.5 18.9 %collective-permute-done.19 = f32[4,16,32,64]{3,2,1,0:T(8,128)S(1)} collective-permute-done((f32[4,16,32,64]{3,2,1,0:T(8,128)S(1)}, f32[4,16,32,64]{3,2,1,0:T(8,128)S(1)}, u32[]{:S(2)}, u32[]{:S(2)}) %collective-permute-start.19) | collective-permute-done | bytes 524320 | tf_op jit(solution)/shard_map/ppermute | solution.py:19
  171.3 7.2 %collective-permute-start.20 = (f32[4,16,32,64]{3,2,1,0:T(8,128)S(1)}, f32[4,16,32,64]{3,2,1,0:T(8,128)S(1)}, u32[]{:S(2)}, u32[]{:S(2)}) collective-permute-start(f32[4,16,32,64]{3,2,1,0:T(8,128)S(1)} %multiply_add_fusion.2), channel_id=1, source_target_pairs={{0,64},{8,72},{16,80},{24,88},{32,96},{40,104},{48,112},{56,120},{... | collective-permute-start | bytes 1572872 | tf_op jit(solution)/shard_map/ppermute | solution.py:19
  180.7 6.6 %fusion.4 = (f32[4,16,128]{2,1,0:T(8,128)}, f32[4,16,128]{2,1,0:T(8,128)}, f32[4,128,128]{1,2,0:T(8,128)S(1)}) fusion(f32[4,16,128]{2,1,0:T(8,128)S(1)} %copy-done.24, f32[4,128,128]{1,2,0:T(8,128)S(1)} %fusion.54, pred[128,128]{0,1:T(8,128)(4,1)S(1)} %copy-done.31, bf16[128,4,16,32]{0,3,2,1:T(8,128)(2,1)S(1)} %bitcast.130, ...), kind=kOutput, calls=%fused_computation.10 | convolution fusion | flops 412270592 | bytes 2244608 | tf_op jit(solution)/shard_map/ctgkp,csgkp->cgkts/dot_general | solution.py:107
  187.3 13.1 %collective-permute-done.20 = f32[4,16,32,64]{3,2,1,0:T(8,128)S(1)} collective-permute-done((f32[4,16,32,64]{3,2,1,0:T(8,128)S(1)}, f32[4,16,32,64]{3,2,1,0:T(8,128)S(1)}, u32[]{:S(2)}, u32[]{:S(2)}) %collective-permute-start.20) | collective-permute-done | bytes 524320 | tf_op jit(solution)/shard_map/ppermute | solution.py:19
  202.2 10.7 %collective-permute-start.21 = (f32[4,16,32,64]{3,2,1,0:T(8,128)}, f32[4,16,32,64]{3,2,1,0:T(8,128)}, u32[]{:S(2)}, u32[]{:S(2)}) collective-permute-start(f32[4,16,32,64]{3,2,1,0:T(8,128)} %multiply_add_fusion.1), channel_id=1, source_target_pairs={{0,136},{8,144},{16,152},{24,160},{32,168},{40,176},{48,184},{56,1... | collective-permute-start | bytes 1572872 | tf_op jit(solution)/shard_map/ppermute | solution.py:19
  214.8 12.6 %collective-permute-done.9 = f32[4,16,32,64]{3,2,1,0:T(8,128)S(1)} collective-permute-done((f32[4,16,32,64]{3,2,1,0:T(8,128)S(1)}, f32[4,16,32,64]{3,2,1,0:T(8,128)S(1)}, u32[]{:S(2)}, u32[]{:S(2)}) %collective-permute-start.9) | collective-permute-done | bytes 524320 | tf_op jit(solution)/shard_map/ppermute | solution.py:19
  233.6 5.0 %fusion.11 = f32[1,128,4,16,32]{1,4,3,2,0:T(8,128)} fusion(bf16[128,4,16,32]{0,3,2,1:T(8,128)(2,1)S(1)} %bitcast.131, f32[4,16,128]{2,1,0:T(8,128)S(1)} %copy-done.24, f32[4,128,128]{1,2,0:T(8,128)S(1)} %fusion.54, pred[128,128]{0,1:T(8,128)(4,1)S(1)} %copy-done.31), kind=kOutput, calls=%fused_computation.17 | convolution fusion | flops 406847488 | bytes 1884160 | tf_op jit(solution)/shard_map/cgkts,ctgkp->csgkp/dot_general | solution.py:108
  246.9 41.2 %collective-permute-done.5 = f32[4,16]{1,0:T(4,128)} collective-permute-done((f32[4,16]{1,0:T(4,128)}, f32[4,16]{1,0:T(4,128)}, u32[]{:S(2)}, u32[]{:S(2)}) %collective-permute-start.5) | collective-permute-done | bytes 288 | tf_op jit(solution)/shard_map/ppermute | solution.py:19
  288.1 3.3 multiply_reduce_fusion.4
  295.3 3.1 multiply_reduce_fusion.5
  298.4 4.2 multiply_reduce_fusion.3
  307.4 106.9 %psum.7 = f32[12928]{0:T(1024)S(1)} all-reduce(f32[12928]{0:T(1024)S(1)} %concatenate.21), channel_id=1, replica_groups=mesh['ctx'=32,'fsdp'=8] {'ctx','fsdp'}, use_global_device_ids=true, to_apply=%region_18.19 | all-reduce | flops 12928 | bytes 103424 | tf_op jit(solution)/shard_map/psum | solution.py:168
  423.3 3.7 fusion.36
  (194 shorter events, 88.7 us)
Async XLA Ops:
  3.4 19.8 %collective-permute-start.1 = (f32[4,16]{1,0:T(4,128)S(1)}, f32[4,16]{1,0:T(4,128)S(1)}, u32[]{:S(2)}, u32[]{:S(2)}) collective-permute-start(f32[4,16]{1,0:T(4,128)S(1)} %exp.91), channel_id=1, source_target_pairs={{8,0},{16,8},{24,16},{32,24},{40,32},{48,40},{56,48},{64,56},{72,6... | collective-permute-start | bytes 776 | tf_op jit(solution)/shard_map/ppermute | solution.py:19
  8.5 14.7 %collective-permute-start.12 = (f32[4,16]{1,0:T(4,128)S(1)}, f32[4,16]{1,0:T(4,128)S(1)}, u32[]{:S(2)}, u32[]{:S(2)}) collective-permute-start(f32[4,16]{1,0:T(4,128)S(1)} %exp.91), channel_id=1, source_target_pairs={{0,8},{8,16},{16,24},{24,32},{32,40},{40,48},{48,56},{56,64},{64,7... | collective-permute-start | bytes 776 | tf_op jit(solution)/shard_map/ppermute | solution.py:19
  13.6 13.2 %all-to-all-start = ((bf16[8,5,320]{2,1,0:T(8,128)(2,1)}), bf16[8,5,320]{2,1,0:T(8,128)(2,1)S(1)}, u32[]{:S(2)}, u32[]{:S(2)}) async-start(bf16[8,5,320]{2,1,0:T(8,128)(2,1)} %stack.12), calls=%async_computation | async-start | bytes 98304 | tf_op jit(solution)/shard_map/all_to_all | solution.py:50
  33.4 27.9 %collective-permute-start.17 = (f32[4,16,32,64]{3,2,1,0:T(8,128)S(1)}, f32[4,16,32,64]{3,2,1,0:T(8,128)S(1)}, u32[]{:S(2)}, u32[]{:S(2)}) collective-permute-start(f32[4,16,32,64]{3,2,1,0:T(8,128)S(1)} %convolution_add_fusion), channel_id=1, source_target_pairs={{0,8},{8,16},{16,24},{24,32},{32,40},{40,48},{48,56},{56,64},{64,7... | collective-permute-start | bytes 1572872 | tf_op jit(solution)/shard_map/ppermute | solution.py:19
  39.4 21.9 %collective-permute-start.6 = (f32[4,16,32,64]{3,2,1,0:T(8,128)S(1)}, f32[4,16,32,64]{3,2,1,0:T(8,128)S(1)}, u32[]{:S(2)}, u32[]{:S(2)}) collective-permute-start(f32[4,16,32,64]{3,2,1,0:T(8,128)S(1)} %convolution_add_fusion.1), channel_id=1, source_target_pairs={{8,0},{16,8},{24,16},{32,24},{40,32},{48,40},{56,48},{64,56},{72,6... | collective-permute-start | bytes 1572872 | tf_op jit(solution)/shard_map/ppermute | solution.py:19
  62.9 77.4 %collective-permute-start.18 = (f32[4,16,32,64]{3,2,1,0:T(8,128)}, f32[4,16,32,64]{3,2,1,0:T(8,128)}, u32[]{:S(2)}, u32[]{:S(2)}) collective-permute-start(f32[4,16,32,64]{3,2,1,0:T(8,128)} %get-tuple-element.86), channel_id=1, source_target_pairs={{0,16},{8,24},{16,32},{24,40},{32,48},{40,56},{48,64},{56,72},{64,... | collective-permute-start | bytes 1572872 | tf_op jit(solution)/shard_map/ppermute | solution.py:19
  65.2 82.7 %collective-permute-start.7 = (f32[4,16,32,64]{3,2,1,0:T(8,128)}, f32[4,16,32,64]{3,2,1,0:T(8,128)}, u32[]{:S(2)}, u32[]{:S(2)}) collective-permute-start(f32[4,16,32,64]{3,2,1,0:T(8,128)} %get-tuple-element.87), channel_id=1, source_target_pairs={{16,0},{24,8},{32,16},{40,24},{48,32},{56,40},{64,48},{72,56},{80,... | collective-permute-start | bytes 1572872 | tf_op jit(solution)/shard_map/ppermute | solution.py:19
  71.5 33.4 %collective-permute-start.13 = (f32[4,16]{1,0:T(4,128)}, f32[4,16]{1,0:T(4,128)}, u32[]{:S(2)}, u32[]{:S(2)}) collective-permute-start(f32[4,16]{1,0:T(4,128)} %get-tuple-element.83), channel_id=1, source_target_pairs={{0,16},{8,24},{16,32},{24,40},{32,48},{40,56},{48,64},{56,72},{64,... | collective-permute-start | bytes 776 | tf_op jit(solution)/shard_map/ppermute | solution.py:19
  81.0 35.5 %collective-permute-start.2 = (f32[4,16]{1,0:T(4,128)}, f32[4,16]{1,0:T(4,128)}, u32[]{:S(2)}, u32[]{:S(2)}) collective-permute-start(f32[4,16]{1,0:T(4,128)} %get-tuple-element.84), channel_id=1, source_target_pairs={{16,0},{24,8},{32,16},{40,24},{48,32},{56,40},{64,48},{72,56},{80,... | collective-permute-start | bytes 776 | tf_op jit(solution)/shard_map/ppermute | solution.py:19
  106.1 13.0 %collective-permute-start.14 = (f32[4,16]{1,0:T(4,128)}, f32[4,16]{1,0:T(4,128)}, u32[]{:S(2)}, u32[]{:S(2)}) collective-permute-start(f32[4,16]{1,0:T(4,128)} %mul.469), channel_id=1, source_target_pairs={{0,32},{8,40},{16,48},{24,56},{32,64},{40,72},{48,80},{56,88},{64,... | collective-permute-start | bytes 776 | tf_op jit(solution)/shard_map/ppermute | solution.py:19
  117.8 7.9 %collective-permute-start.3 = (f32[4,16]{1,0:T(4,128)}, f32[4,16]{1,0:T(4,128)}, u32[]{:S(2)}, u32[]{:S(2)}) collective-permute-start(f32[4,16]{1,0:T(4,128)} %mul.440), channel_id=1, source_target_pairs={{32,0},{40,8},{48,16},{56,24},{64,32},{72,40},{80,48},{88,56},{96,... | collective-permute-start | bytes 776 | tf_op jit(solution)/shard_map/ppermute | solution.py:19
  120.4 7.9 %collective-permute-start.15 = (f32[4,16]{1,0:T(4,128)}, f32[4,16]{1,0:T(4,128)}, u32[]{:S(2)}, u32[]{:S(2)}) collective-permute-start(f32[4,16]{1,0:T(4,128)} %mul.470), channel_id=1, source_target_pairs={{0,64},{8,72},{16,80},{24,88},{32,96},{40,104},{48,112},{56,120},{... | collective-permute-start | bytes 776 | tf_op jit(solution)/shard_map/ppermute | solution.py:19
  127.0 12.1 %collective-permute-start.4 = (f32[4,16]{1,0:T(4,128)}, f32[4,16]{1,0:T(4,128)}, u32[]{:S(2)}, u32[]{:S(2)}) collective-permute-start(f32[4,16]{1,0:T(4,128)} %mul.441), channel_id=1, source_target_pairs={{64,0},{72,8},{80,16},{88,24},{96,32},{104,40},{112,48},{120,56},{... | collective-permute-start | bytes 776 | tf_op jit(solution)/shard_map/ppermute | solution.py:19
  129.0 111.9 %collective-permute-start.16 = (f32[4,16]{1,0:T(4,128)S(1)}, f32[4,16]{1,0:T(4,128)}, u32[]{:S(2)}, u32[]{:S(2)}) collective-permute-start(f32[4,16]{1,0:T(4,128)S(1)} %mul.471), channel_id=1, source_target_pairs={{0,8},{8,16},{16,24},{24,32},{32,40},{40,48},{48,56},{56,64},{64,7... | collective-permute-start | bytes 776 | tf_op jit(solution)/shard_map/ppermute | solution.py:19
  142.0 28.4 %collective-permute-start.19 = (f32[4,16,32,64]{3,2,1,0:T(8,128)S(1)}, f32[4,16,32,64]{3,2,1,0:T(8,128)S(1)}, u32[]{:S(2)}, u32[]{:S(2)}) collective-permute-start(f32[4,16,32,64]{3,2,1,0:T(8,128)S(1)} %multiply_add_fusion.3), channel_id=1, source_target_pairs={{0,32},{8,40},{16,48},{24,56},{32,64},{40,72},{48,80},{56,88},{64,... | collective-permute-start | bytes 1572872 | tf_op jit(solution)/shard_map/ppermute | solution.py:19
  149.6 28.9 %collective-permute-start.8 = (f32[4,16,32,64]{3,2,1,0:T(8,128)S(1)}, f32[4,16,32,64]{3,2,1,0:T(8,128)S(1)}, u32[]{:S(2)}, u32[]{:S(2)}) collective-permute-start(f32[4,16,32,64]{3,2,1,0:T(8,128)S(1)} %multiply_add_fusion.10), channel_id=1, source_target_pairs={{32,0},{40,8},{48,16},{56,24},{64,32},{72,40},{80,48},{88,56},{96,... | collective-permute-start | bytes 1572872 | tf_op jit(solution)/shard_map/ppermute | solution.py:19
  171.3 29.1 %collective-permute-start.20 = (f32[4,16,32,64]{3,2,1,0:T(8,128)S(1)}, f32[4,16,32,64]{3,2,1,0:T(8,128)S(1)}, u32[]{:S(2)}, u32[]{:S(2)}) collective-permute-start(f32[4,16,32,64]{3,2,1,0:T(8,128)S(1)} %multiply_add_fusion.2), channel_id=1, source_target_pairs={{0,64},{8,72},{16,80},{24,88},{32,96},{40,104},{48,112},{56,120},{... | collective-permute-start | bytes 1572872 | tf_op jit(solution)/shard_map/ppermute | solution.py:19
  179.3 48.0 %collective-permute-start.9 = (f32[4,16,32,64]{3,2,1,0:T(8,128)S(1)}, f32[4,16,32,64]{3,2,1,0:T(8,128)S(1)}, u32[]{:S(2)}, u32[]{:S(2)}) collective-permute-start(f32[4,16,32,64]{3,2,1,0:T(8,128)S(1)} %multiply_add_fusion.9), channel_id=1, source_target_pairs={{64,0},{72,8},{80,16},{88,24},{96,32},{104,40},{112,48},{120,56},{... | collective-permute-start | bytes 1572872 | tf_op jit(solution)/shard_map/ppermute | solution.py:19
  202.2 85.8 %collective-permute-start.21 = (f32[4,16,32,64]{3,2,1,0:T(8,128)}, f32[4,16,32,64]{3,2,1,0:T(8,128)}, u32[]{:S(2)}, u32[]{:S(2)}) collective-permute-start(f32[4,16,32,64]{3,2,1,0:T(8,128)} %multiply_add_fusion.1), channel_id=1, source_target_pairs={{0,136},{8,144},{16,152},{24,160},{32,168},{40,176},{48,184},{56,1... | collective-permute-start | bytes 1572872 | tf_op jit(solution)/shard_map/ppermute | solution.py:19
  212.9 75.1 %collective-permute-start.22 = (f32[4,16,32,64]{3,2,1,0:T(8,128)}, f32[4,16,32,64]{3,2,1,0:T(8,128)}, u32[]{:S(2)}, u32[]{:S(2)}) collective-permute-start(f32[4,16,32,64]{3,2,1,0:T(8,128)} %multiply_add_fusion.1), channel_id=1, source_target_pairs={{0,8},{8,16},{16,24},{24,32},{32,40},{40,48},{48,56},{56,64},{64,7... | collective-permute-start | bytes 1572872 | tf_op jit(solution)/shard_map/ppermute | solution.py:19
  229.3 58.8 %collective-permute-start.10 = (f32[4,16,32,64]{3,2,1,0:T(8,128)}, f32[4,16,32,64]{3,2,1,0:T(8,128)}, u32[]{:S(2)}, u32[]{:S(2)}) collective-permute-start(f32[4,16,32,64]{3,2,1,0:T(8,128)} %multiply_add_fusion.8), channel_id=1, source_target_pairs={{136,0},{144,8},{152,16},{160,24},{168,32},{176,40},{184,48},{192,... | collective-permute-start | bytes 1572872 | tf_op jit(solution)/shard_map/ppermute | solution.py:19
  230.6 57.5 %collective-permute-start.11 = (f32[4,16,32,64]{3,2,1,0:T(8,128)}, f32[4,16,32,64]{3,2,1,0:T(8,128)}, u32[]{:S(2)}, u32[]{:S(2)}) collective-permute-start(f32[4,16,32,64]{3,2,1,0:T(8,128)} %multiply_add_fusion.8), channel_id=1, source_target_pairs={{8,0},{16,8},{24,16},{32,24},{40,32},{48,40},{56,48},{64,56},{72,6... | collective-permute-start | bytes 1572872 | tf_op jit(solution)/shard_map/ppermute | solution.py:19
  240.9 47.2 %collective-permute-start.5 = (f32[4,16]{1,0:T(4,128)}, f32[4,16]{1,0:T(4,128)}, u32[]{:S(2)}, u32[]{:S(2)}) collective-permute-start(f32[4,16]{1,0:T(4,128)} %mul.442), channel_id=1, source_target_pairs={{8,0},{16,8},{24,16},{32,24},{40,32},{48,40},{56,48},{64,56},{72,6... | collective-permute-start | bytes 776 | tf_op jit(solution)/shard_map/ppermute | solution.py:19
  416.0 6.8 %collective-permute-start.23 = (f32[3,2560]{1,0:T(4,128)S(1)}, f32[3,2560]{1,0:T(4,128)S(1)}, u32[]{:S(2)}, u32[]{:S(2)}) collective-permute-start(f32[3,2560]{1,0:T(4,128)S(1)} %copy.142), channel_id=1, source_target_pairs={{8,0},{16,8},{24,16},{32,24},{40,32},{48,40},{56,48},{64,56},{72,6... | collective-permute-start | bytes 92168 | tf_op jit(solution)/shard_map/ppermute | solution.py:19
  (39 other events, 462.8 us)
